TPU v7x, 512 devices: a whole 4x4x16 slice. The times are simulated.
512 devices in a mesh: seq: 16 (over x, y_hi, core), shard: 32 (over y_lo, z).
Axes of the slice: x: 4, y: 4 (y_hi: 2, y_lo: 2; y = y_hi * 2 + y_lo), z: 16, core: 2. Of those that a mesh axis runs over, the one named last changes fastest.
Arguments:
- features: bfloat16 [4096, 4096], P('seq', 'shard'), may hold values from -6 to 6
- in_proj: bfloat16 [4096, 3, 4096], P(None, None, 'shard'), may hold values from -0.09375 to 0.09375
- short_filter: float32 [3, 3, 4096], replicated, may hold values from -3.5 to 3.5
- residue: float32 [16, 4096], P(None, 'shard'), may hold values from -1.5 to 1.5
- decay_rate: float32 [16, 4096], P(None, 'shard'), may hold values from 0.05 to 1000
- skip_gain: float32 [4096], P('shard'), may hold values from -4 to 4
Outputs:
- gated: bfloat16 [4096, 4096], P('seq', 'shard')
All inputs are finite; a program needn't handle non-finite values.
Results may differ from a plain program's by a relative error of at most 0.0063.
Values may be sent and summed in bfloat16 or wider, within the bound.
No kernel may reach another device: no remote copies, remote signals or barrier semaphores. Data moves between devices by JAX's collectives and lax.ppermute only.
A program may use at most 64 MiB of HBM per device.

v0:
```python
import math
import jax
import jax.numpy as jnp
from jax import lax
from jax.sharding import PartitionSpec as P


def shifted(value, axis, steps):
    count = lax.axis_size(axis)
    initial, last = (max(0, -steps), min(count, count - steps))
    return lax.ppermute(value, axis, [(source, source + steps) for source in range(initial, last)])


def mode_tables(residue, decay_rate, total_len, block_len):
    step_rate = decay_rate / total_len
    mode_gain = residue * jnp.sqrt(jnp.expm1(-2.0 * step_rate) / jnp.expm1(-2.0 * decay_rate))
    steps = jnp.arange(block_len, dtype=jnp.float32)[:, None, None]
    lagged = jnp.exp(-step_rate * steps)
    kernel = jnp.sum(mode_gain * lagged, axis=1)
    offsets = jnp.arange(block_len)[:, None] - jnp.arange(block_len)[None, :]
    toeplitz = jnp.where(
        (offsets >= 0)[:, :, None], kernel[jnp.clip(offsets, 0, block_len - 1)], 0.0
    )
    head_table = mode_gain * jnp.exp(-step_rate * (steps + 1.0))
    tail_table = jnp.exp(-step_rate * (block_len - 1.0 - steps))
    step_decay = jnp.exp(-step_rate * block_len)
    return (toeplitz, head_table, tail_table, step_decay)


def project_rows(row_block, w_flat):
    return jnp.dot(
        lax.all_gather(row_block, "shard", axis=1, tiled=True),
        w_flat,
        preferred_element_type=jnp.float32,
    )


def shards(features, in_proj, short_filter, residue, decay_rate, skip_gain):
    length = features.shape[0]
    channels = in_proj.shape[2]
    tap_count = short_filter.shape[0]
    rim_count = tap_count - 1
    seq_count = lax.axis_size("seq")
    total_len = length * seq_count
    w_flat = in_proj.reshape(in_proj.shape[0], 3 * channels)
    proj = project_rows(features, w_flat).astype(jnp.bfloat16).reshape(length, 3, channels)
    rim_rows = shifted(proj[length - rim_count :], "seq", 1)
    extended = jnp.concatenate([rim_rows, proj], 0)
    extended = extended.astype(jnp.float32)
    own_taps = lax.dynamic_slice_in_dim(
        short_filter, lax.axis_index("shard") * channels, channels, 2
    )
    filtered = jnp.zeros((length, 3, channels), jnp.float32)
    for tap_index in range(tap_count):
        start_row = rim_count - tap_index
        filtered = filtered + own_taps[tap_index] * extended[start_row : start_row + length]
    drive_term = filtered[:, 1, :] * filtered[:, 2, :]
    block_len = math.gcd(length, 128)
    block_count = length // block_len
    toeplitz, head_table, tail_table, step_decay = mode_tables(
        residue, decay_rate, total_len, block_len
    )
    highest = lax.Precision.HIGHEST
    blocks = drive_term.reshape(block_count, block_len, channels)
    intra = jnp.einsum("tsc,bsc->btc", toeplitz, blocks, precision=highest)
    states = jnp.einsum("bsc,smc->bmc", blocks, tail_table, precision=highest)

    def accumulate(carried, state_in):
        return (carried * step_decay + state_in, carried)

    total_state, carries = lax.scan(accumulate, jnp.zeros(residue.shape, jnp.float32), states)
    device_decay = jnp.exp(-(decay_rate / total_len) * length)

    def relay(turn, incoming):
        return shifted(incoming * device_decay + total_state, "seq", 1)

    incoming = lax.fori_loop(0, seq_count - 1, relay, jnp.zeros_like(total_state))
    block_starts = (block_len * jnp.arange(block_count, dtype=jnp.float32))[:, None, None]
    entering = carries + jnp.exp(-(decay_rate / total_len)[None] * block_starts) * incoming[None]
    correction = jnp.einsum("tmc,bmc->btc", head_table, entering, precision=highest)
    longconv = (intra + correction).reshape(length, channels)
    return (filtered[:, 0, :] * (longconv + skip_gain * drive_term)).astype(jnp.bfloat16)


def solution(mesh):
    placed = (
        P("seq", "shard"),
        P(None, None, "shard"),
        P(),
        P(None, "shard"),
        P(None, "shard"),
        P("shard"),
    )
    return jax.shard_map(
        shards, mesh=mesh, in_specs=placed, out_specs=P("seq", "shard"), check_vma=False
    )
```

profile of v0, /device:TPU:2, one launch (start us, length us, event | category | flops | bytes accessed | tf_op | source)
XLA Modules:
  0.0 349.9 jit_solution(4702001722327481454)
XLA Ops:
  6.5 0.7 all-gather.2.cloned.1.call-update
  7.3 3.2 copy.26
  10.5 0.7 sqrt_multiply_fusion
  11.5 0.7 dynamic-slice_bitcast_fusion.2
  12.2 1.2 multiply_reduce_fusion
  13.5 128.5 %all-gather.2.cloned.1.call-done = bf16[256,4096]{1,0:T(8,128)(2,1)} async-done(((bf16[256,128]{1,0:T(8,128)(2,1)}), bf16[256,4096]{1,0:T(8,128)(2,1)}) %all-gather.2.cloned.1.call-update) | async-done | bytes 2097168 | tf_op jit(solution)/shard_map/all_gather | solution.py:32
  142.0 2.9 convolution_convert_fusion
  144.9 1.9 collective-permute-start.1
  146.8 0.9 copy.31
  147.8 54.5 %gather_fusion = f32[16384,128]{1,0:T(8,128)} fusion(f32[128,128]{1,0:T(8,128)S(1)} %copy.31, s32[16384]{0:T(1024)S(1)} %fusion.23), kind=kCustom, calls=%fused_computation | custom fusion | bytes 16842752 | tf_op jit(solution)/shard_map/gather | solution.py:22
  202.3 9.4 %copy.32 = f32[128,128,128]{1,0,2:T(8,128)} copy(f32[128,128,128]{2,1,0:T(8,128)} %bitcast.48) | data formatting | bytes 16777216 | tf_op jit(solution)/shard_map/gather | solution.py:22
  211.8 0.2 copy.28
  212.1 0.4 fusion.18
  212.7 1.9 convolution_bitcast_fusion
  214.7 110.5 %while.23 = (s32[]{:T(128)}, f32[16,128]{1,0:T(8,128)S(1)}, f32[16,128]{1,0:T(8,128)S(1)}, f32[16,128]{1,0:T(8,128)S(1)}, s32[]{:T(128)}) while((s32[]{:T(128)}, f32[16,128]{1,0:T(8,128)S(1)}, f32[16,128]{1,0:T(8,128)S(1)}, f32[16,128]{1,0:T(8,128)S(1)}, s32[]{:T(128)}) %tuple.46), condition=%wide.region_4.5_spmd, body=%wide.region_3.4_spmd.sunk | while | flops 4098 | bytes 65637 | solution.py:77
  214.7 5.1 %collective-permute-start = (f32[16,128]{1,0:T(8,128)S(1)}, f32[16,128]{1,0:T(8,128)S(1)}, u32[]{:S(2)}, u32[]{:S(2)}) collective-permute-start(f32[16,128]{1,0:T(8,128)S(1)} %multiply_add_fusion.3), channel_id=1, source_target_pairs={{0,32},{32,64},{64,96},{96,128},{128,160},{160,192},{192,224},{224... | collective-permute-start | bytes 24584 | tf_op jit(solution)/shard_map/while/body/eval_jaxpr/ppermute | solution.py:11
  219.9 2.2 collective-permute-done
  222.1 1.9 collective-permute-start
  224.0 5.4 %collective-permute-done = f32[16,128]{1,0:T(8,128)S(1)} collective-permute-done((f32[16,128]{1,0:T(8,128)S(1)}, f32[16,128]{1,0:T(8,128)S(1)}, u32[]{:S(2)}, u32[]{:S(2)}) %collective-permute-start) | collective-permute-done | bytes 8224 | tf_op jit(solution)/shard_map/while/body/eval_jaxpr/ppermute | solution.py:11
  229.5 1.9 collective-permute-start
  231.4 5.4 %collective-permute-done = f32[16,128]{1,0:T(8,128)S(1)} collective-permute-done((f32[16,128]{1,0:T(8,128)S(1)}, f32[16,128]{1,0:T(8,128)S(1)}, u32[]{:S(2)}, u32[]{:S(2)}) %collective-permute-start) | collective-permute-done | bytes 8224 | tf_op jit(solution)/shard_map/while/body/eval_jaxpr/ppermute | solution.py:11
  236.8 1.9 collective-permute-start
  238.8 5.4 %collective-permute-done = f32[16,128]{1,0:T(8,128)S(1)} collective-permute-done((f32[16,128]{1,0:T(8,128)S(1)}, f32[16,128]{1,0:T(8,128)S(1)}, u32[]{:S(2)}, u32[]{:S(2)}) %collective-permute-start) | collective-permute-done | bytes 8224 | tf_op jit(solution)/shard_map/while/body/eval_jaxpr/ppermute | solution.py:11
  244.2 1.9 collective-permute-start
  246.1 5.4 %collective-permute-done = f32[16,128]{1,0:T(8,128)S(1)} collective-permute-done((f32[16,128]{1,0:T(8,128)S(1)}, f32[16,128]{1,0:T(8,128)S(1)}, u32[]{:S(2)}, u32[]{:S(2)}) %collective-permute-start) | collective-permute-done | bytes 8224 | tf_op jit(solution)/shard_map/while/body/eval_jaxpr/ppermute | solution.py:11
  251.6 1.9 collective-permute-start
  253.5 5.4 %collective-permute-done = f32[16,128]{1,0:T(8,128)S(1)} collective-permute-done((f32[16,128]{1,0:T(8,128)S(1)}, f32[16,128]{1,0:T(8,128)S(1)}, u32[]{:S(2)}, u32[]{:S(2)}) %collective-permute-start) | collective-permute-done | bytes 8224 | tf_op jit(solution)/shard_map/while/body/eval_jaxpr/ppermute | solution.py:11
  258.9 1.9 collective-permute-start
  260.9 5.4 %collective-permute-done = f32[16,128]{1,0:T(8,128)S(1)} collective-permute-done((f32[16,128]{1,0:T(8,128)S(1)}, f32[16,128]{1,0:T(8,128)S(1)}, u32[]{:S(2)}, u32[]{:S(2)}) %collective-permute-start) | collective-permute-done | bytes 8224 | tf_op jit(solution)/shard_map/while/body/eval_jaxpr/ppermute | solution.py:11
  266.3 1.9 collective-permute-start
  268.2 5.4 %collective-permute-done = f32[16,128]{1,0:T(8,128)S(1)} collective-permute-done((f32[16,128]{1,0:T(8,128)S(1)}, f32[16,128]{1,0:T(8,128)S(1)}, u32[]{:S(2)}, u32[]{:S(2)}) %collective-permute-start) | collective-permute-done | bytes 8224 | tf_op jit(solution)/shard_map/while/body/eval_jaxpr/ppermute | solution.py:11
  273.7 1.9 collective-permute-start
  275.6 5.4 %collective-permute-done = f32[16,128]{1,0:T(8,128)S(1)} collective-permute-done((f32[16,128]{1,0:T(8,128)S(1)}, f32[16,128]{1,0:T(8,128)S(1)}, u32[]{:S(2)}, u32[]{:S(2)}) %collective-permute-start) | collective-permute-done | bytes 8224 | tf_op jit(solution)/shard_map/while/body/eval_jaxpr/ppermute | solution.py:11
  281.0 1.9 collective-permute-start
  283.0 5.4 %collective-permute-done = f32[16,128]{1,0:T(8,128)S(1)} collective-permute-done((f32[16,128]{1,0:T(8,128)S(1)}, f32[16,128]{1,0:T(8,128)S(1)}, u32[]{:S(2)}, u32[]{:S(2)}) %collective-permute-start) | collective-permute-done | bytes 8224 | tf_op jit(solution)/shard_map/while/body/eval_jaxpr/ppermute | solution.py:11
  288.4 1.9 collective-permute-start
  290.3 5.4 %collective-permute-done = f32[16,128]{1,0:T(8,128)S(1)} collective-permute-done((f32[16,128]{1,0:T(8,128)S(1)}, f32[16,128]{1,0:T(8,128)S(1)}, u32[]{:S(2)}, u32[]{:S(2)}) %collective-permute-start) | collective-permute-done | bytes 8224 | tf_op jit(solution)/shard_map/while/body/eval_jaxpr/ppermute | solution.py:11
  295.8 1.9 collective-permute-start
  297.7 5.4 %collective-permute-done = f32[16,128]{1,0:T(8,128)S(1)} collective-permute-done((f32[16,128]{1,0:T(8,128)S(1)}, f32[16,128]{1,0:T(8,128)S(1)}, u32[]{:S(2)}, u32[]{:S(2)}) %collective-permute-start) | collective-permute-done | bytes 8224 | tf_op jit(solution)/shard_map/while/body/eval_jaxpr/ppermute | solution.py:11
  303.1 1.9 collective-permute-start
  305.1 5.4 %collective-permute-done = f32[16,128]{1,0:T(8,128)S(1)} collective-permute-done((f32[16,128]{1,0:T(8,128)S(1)}, f32[16,128]{1,0:T(8,128)S(1)}, u32[]{:S(2)}, u32[]{:S(2)}) %collective-permute-start) | collective-permute-done | bytes 8224 | tf_op jit(solution)/shard_map/while/body/eval_jaxpr/ppermute | solution.py:11
  310.5 1.9 collective-permute-start
  312.4 5.4 %collective-permute-done = f32[16,128]{1,0:T(8,128)S(1)} collective-permute-done((f32[16,128]{1,0:T(8,128)S(1)}, f32[16,128]{1,0:T(8,128)S(1)}, u32[]{:S(2)}, u32[]{:S(2)}) %collective-permute-start) | collective-permute-done | bytes 8224 | tf_op jit(solution)/shard_map/while/body/eval_jaxpr/ppermute | solution.py:11
  317.9 1.9 collective-permute-start
  319.8 5.4 %collective-permute-done = f32[16,128]{1,0:T(8,128)S(1)} collective-permute-done((f32[16,128]{1,0:T(8,128)S(1)}, f32[16,128]{1,0:T(8,128)S(1)}, u32[]{:S(2)}, u32[]{:S(2)}) %collective-permute-start) | collective-permute-done | bytes 8224 | tf_op jit(solution)/shard_map/while/body/eval_jaxpr/ppermute | solution.py:11
  325.4 1.4 fusion.7
  326.8 15.4 %fusion.4 = f32[128,2,128]{2,1,0:T(2,128)S(1)} fusion(f32[128,2,128]{2,1,0:T(2,128)S(1)} %fusion.7, f32[2,128,128]{1,0,2:T(2,128)S(1)} %mul.171, f32[128,128,128]{1,0,2:T(8,128)} %copy.32, pred[128,128]{1,0:T(8,128)(4,1)S(1)} %subtract_compare_fusion), kind=kOutput, calls=%fused_computation.9 | convolution fusion | flops 52461568 | bytes 8798208 | tf_op jit(solution)/shard_map/tsc,bsc->btc/dot_general | solution.py:65
  342.4 0.7 copy.35
  (48 shorter events, 1.3 us)
Async XLA Ops:
  6.5 135.4 %all-gather.2.cloned.1.call-start = ((), (), s32[]{:S(2)}) async-start(), calls=%async_computation | async-start | bytes 2162688 | tf_op jit(solution)/shard_map/all_gather | solution.py:32
  11.4 0.8 copy-start
  144.9 66.9 %collective-permute-start.1 = (bf16[2,3,128]{2,1,0:T(4,128)(2,1)S(1)}, bf16[2,3,128]{2,1,0:T(4,128)(2,1)S(1)}, u32[]{:S(2)}, u32[]{:S(2)}) collective-permute-start(bf16[2,3,128]{2,1,0:T(4,128)(2,1)S(1)} %slice.35), channel_id=1, source_target_pairs={{0,32},{32,64},{64,96},{96,128},{128,160},{160,192},{192,224},{224... | collective-permute-start | bytes 4616 | tf_op jit(solution)/shard_map/ppermute | solution.py:11
  202.3 123.2 %copy-start.1 = (f32[16,128]{0,1:T(8,128)S(1)}, f32[16,128]{0,1:T(8,128)}, u32[]{:S(2)}) copy-start(f32[16,128]{0,1:T(8,128)} %copy-done) | copy-start | bytes 24580
  211.6 130.6 %copy-start.2 = (f32[128]{0:T(128)S(1)}, f32[128]{0:T(128)}, u32[]{:S(2)}) copy-start(f32[128]{0:T(128)} %param.15) | copy-start | bytes 1540
  214.7 7.4 %collective-permute-start = (f32[16,128]{1,0:T(8,128)S(1)}, f32[16,128]{1,0:T(8,128)S(1)}, u32[]{:S(2)}, u32[]{:S(2)}) collective-permute-start(f32[16,128]{1,0:T(8,128)S(1)} %multiply_add_fusion.3), channel_id=1, source_target_pairs={{0,32},{32,64},{64,96},{96,128},{128,160},{160,192},{192,224},{224... | collective-permute-start | bytes 24584 | tf_op jit(solution)/shard_map/while/body/eval_jaxpr/ppermute | solution.py:11
  222.1 7.4 %collective-permute-start = (f32[16,128]{1,0:T(8,128)S(1)}, f32[16,128]{1,0:T(8,128)S(1)}, u32[]{:S(2)}, u32[]{:S(2)}) collective-permute-start(f32[16,128]{1,0:T(8,128)S(1)} %multiply_add_fusion.3), channel_id=1, source_target_pairs={{0,32},{32,64},{64,96},{96,128},{128,160},{160,192},{192,224},{224... | collective-permute-start | bytes 24584 | tf_op jit(solution)/shard_map/while/body/eval_jaxpr/ppermute | solution.py:11
  229.5 7.4 %collective-permute-start = (f32[16,128]{1,0:T(8,128)S(1)}, f32[16,128]{1,0:T(8,128)S(1)}, u32[]{:S(2)}, u32[]{:S(2)}) collective-permute-start(f32[16,128]{1,0:T(8,128)S(1)} %multiply_add_fusion.3), channel_id=1, source_target_pairs={{0,32},{32,64},{64,96},{96,128},{128,160},{160,192},{192,224},{224... | collective-permute-start | bytes 24584 | tf_op jit(solution)/shard_map/while/body/eval_jaxpr/ppermute | solution.py:11
  236.8 7.4 %collective-permute-start = (f32[16,128]{1,0:T(8,128)S(1)}, f32[16,128]{1,0:T(8,128)S(1)}, u32[]{:S(2)}, u32[]{:S(2)}) collective-permute-start(f32[16,128]{1,0:T(8,128)S(1)} %multiply_add_fusion.3), channel_id=1, source_target_pairs={{0,32},{32,64},{64,96},{96,128},{128,160},{160,192},{192,224},{224... | collective-permute-start | bytes 24584 | tf_op jit(solution)/shard_map/while/body/eval_jaxpr/ppermute | solution.py:11
  244.2 7.4 %collective-permute-start = (f32[16,128]{1,0:T(8,128)S(1)}, f32[16,128]{1,0:T(8,128)S(1)}, u32[]{:S(2)}, u32[]{:S(2)}) collective-permute-start(f32[16,128]{1,0:T(8,128)S(1)} %multiply_add_fusion.3), channel_id=1, source_target_pairs={{0,32},{32,64},{64,96},{96,128},{128,160},{160,192},{192,224},{224... | collective-permute-start | bytes 24584 | tf_op jit(solution)/shard_map/while/body/eval_jaxpr/ppermute | solution.py:11
  251.6 7.4 %collective-permute-start = (f32[16,128]{1,0:T(8,128)S(1)}, f32[16,128]{1,0:T(8,128)S(1)}, u32[]{:S(2)}, u32[]{:S(2)}) collective-permute-start(f32[16,128]{1,0:T(8,128)S(1)} %multiply_add_fusion.3), channel_id=1, source_target_pairs={{0,32},{32,64},{64,96},{96,128},{128,160},{160,192},{192,224},{224... | collective-permute-start | bytes 24584 | tf_op jit(solution)/shard_map/while/body/eval_jaxpr/ppermute | solution.py:11
  258.9 7.4 %collective-permute-start = (f32[16,128]{1,0:T(8,128)S(1)}, f32[16,128]{1,0:T(8,128)S(1)}, u32[]{:S(2)}, u32[]{:S(2)}) collective-permute-start(f32[16,128]{1,0:T(8,128)S(1)} %multiply_add_fusion.3), channel_id=1, source_target_pairs={{0,32},{32,64},{64,96},{96,128},{128,160},{160,192},{192,224},{224... | collective-permute-start | bytes 24584 | tf_op jit(solution)/shard_map/while/body/eval_jaxpr/ppermute | solution.py:11
  266.3 7.4 %collective-permute-start = (f32[16,128]{1,0:T(8,128)S(1)}, f32[16,128]{1,0:T(8,128)S(1)}, u32[]{:S(2)}, u32[]{:S(2)}) collective-permute-start(f32[16,128]{1,0:T(8,128)S(1)} %multiply_add_fusion.3), channel_id=1, source_target_pairs={{0,32},{32,64},{64,96},{96,128},{128,160},{160,192},{192,224},{224... | collective-permute-start | bytes 24584 | tf_op jit(solution)/shard_map/while/body/eval_jaxpr/ppermute | solution.py:11
  273.7 7.4 %collective-permute-start = (f32[16,128]{1,0:T(8,128)S(1)}, f32[16,128]{1,0:T(8,128)S(1)}, u32[]{:S(2)}, u32[]{:S(2)}) collective-permute-start(f32[16,128]{1,0:T(8,128)S(1)} %multiply_add_fusion.3), channel_id=1, source_target_pairs={{0,32},{32,64},{64,96},{96,128},{128,160},{160,192},{192,224},{224... | collective-permute-start | bytes 24584 | tf_op jit(solution)/shard_map/while/body/eval_jaxpr/ppermute | solution.py:11
  281.0 7.4 %collective-permute-start = (f32[16,128]{1,0:T(8,128)S(1)}, f32[16,128]{1,0:T(8,128)S(1)}, u32[]{:S(2)}, u32[]{:S(2)}) collective-permute-start(f32[16,128]{1,0:T(8,128)S(1)} %multiply_add_fusion.3), channel_id=1, source_target_pairs={{0,32},{32,64},{64,96},{96,128},{128,160},{160,192},{192,224},{224... | collective-permute-start | bytes 24584 | tf_op jit(solution)/shard_map/while/body/eval_jaxpr/ppermute | solution.py:11
  288.4 7.4 %collective-permute-start = (f32[16,128]{1,0:T(8,128)S(1)}, f32[16,128]{1,0:T(8,128)S(1)}, u32[]{:S(2)}, u32[]{:S(2)}) collective-permute-start(f32[16,128]{1,0:T(8,128)S(1)} %multiply_add_fusion.3), channel_id=1, source_target_pairs={{0,32},{32,64},{64,96},{96,128},{128,160},{160,192},{192,224},{224... | collective-permute-start | bytes 24584 | tf_op jit(solution)/shard_map/while/body/eval_jaxpr/ppermute | solution.py:11
  295.8 7.4 %collective-permute-start = (f32[16,128]{1,0:T(8,128)S(1)}, f32[16,128]{1,0:T(8,128)S(1)}, u32[]{:S(2)}, u32[]{:S(2)}) collective-permute-start(f32[16,128]{1,0:T(8,128)S(1)} %multiply_add_fusion.3), channel_id=1, source_target_pairs={{0,32},{32,64},{64,96},{96,128},{128,160},{160,192},{192,224},{224... | collective-permute-start | bytes 24584 | tf_op jit(solution)/shard_map/while/body/eval_jaxpr/ppermute | solution.py:11
  303.1 7.4 %collective-permute-start = (f32[16,128]{1,0:T(8,128)S(1)}, f32[16,128]{1,0:T(8,128)S(1)}, u32[]{:S(2)}, u32[]{:S(2)}) collective-permute-start(f32[16,128]{1,0:T(8,128)S(1)} %multiply_add_fusion.3), channel_id=1, source_target_pairs={{0,32},{32,64},{64,96},{96,128},{128,160},{160,192},{192,224},{224... | collective-permute-start | bytes 24584 | tf_op jit(solution)/shard_map/while/body/eval_jaxpr/ppermute | solution.py:11
  310.5 7.4 %collective-permute-start = (f32[16,128]{1,0:T(8,128)S(1)}, f32[16,128]{1,0:T(8,128)S(1)}, u32[]{:S(2)}, u32[]{:S(2)}) collective-permute-start(f32[16,128]{1,0:T(8,128)S(1)} %multiply_add_fusion.3), channel_id=1, source_target_pairs={{0,32},{32,64},{64,96},{96,128},{128,160},{160,192},{192,224},{224... | collective-permute-start | bytes 24584 | tf_op jit(solution)/shard_map/while/body/eval_jaxpr/ppermute | solution.py:11
  317.9 7.4 %collective-permute-start = (f32[16,128]{1,0:T(8,128)S(1)}, f32[16,128]{1,0:T(8,128)S(1)}, u32[]{:S(2)}, u32[]{:S(2)}) collective-permute-start(f32[16,128]{1,0:T(8,128)S(1)} %multiply_add_fusion.3), channel_id=1, source_target_pairs={{0,32},{32,64},{64,96},{96,128},{128,160},{160,192},{192,224},{224... | collective-permute-start | bytes 24584 | tf_op jit(solution)/shard_map/while/body/eval_jaxpr/ppermute | solution.py:11
Sparse Core Ops, SparseCore 0:
  9.4 132.5 all-gather.1
where the time goes:
time: 351 us; the launch traced here: 350 us
  waiting for transfers between devices  208 us (59%)
  local copies, waits for them, and re-layouts  70.3 us (20%)
  starting transfers between devices  33.8 us (10%)
  matrix products  21.5 us (6%)
  between operations  13.6 us (4%)
    all_gather x1, waiting for transfers between devices, project_rows(): lax.all_gather(row_block, 'shard', axis=1, tiled=True)  128 us
    ppermute x16, waiting for transfers between devices, shifted(): lax.ppermute(value, axis, [(source, source + steps) for source in range(i...  78.4 us
    gather x2, local copies, waits for them, and re-layouts, mode_tables(): kernel[jnp.clip(offsets, 0, block_len - 1)]  63.9 us
    ppermute x16, starting transfers between devices, shifted(): lax.ppermute(value, axis, [(source, source + steps) for source in range(i...  33.8 us
    dot_general x1, matrix products, shards(): intra = jnp.einsum('tsc,bsc->btc', toeplitz, blocks, precision=highest)  15.4 us
  transfers between devices with their start and end apart: 17, of which 16 were waited for; matrix products, arithmetic and copies ran while one was open for 20% of the time, Pallas kernels for 0%

commit v1 on v0

--- a/solution.py
+++ b/solution.py
@@ -3,6 +3,7 @@
 import jax.numpy as jnp
 from jax import lax
 from jax.sharding import PartitionSpec as P
+from jax.lax import all_to_all, axis_size
 
 
 def shifted(value, axis, steps):
@@ -29,7 +30,15 @@
 
 def project_rows(row_block, w_flat):
     return jnp.dot(
-        lax.all_gather(row_block, "shard", axis=1, tiled=True),
+        jnp.concatenate(
+            all_to_all(
+                jnp.stack([row_block] * axis_size("shard"), 0),
+                concat_axis=0,
+                axis_name="shard",
+                split_axis=0,
+            ),
+            1,
+        ),
         w_flat,
         preferred_element_type=jnp.float32,
     )

time: 351 us -> 321 us (0.915)
  the two profiles are of different devices: /device:TPU:2 before, /device:TPU:38 now
where the time goes in v1:
time: 321 us; the launch traced here: 320 us
  waiting for transfers between devices  174 us (54%)
  local copies, waits for them, and re-layouts  71.6 us (22%)
  starting transfers between devices  50.3 us (16%)
  matrix products  22.5 us (7%)
    all_to_all x1, waiting for transfers between devices, project_rows(): all_to_all(jnp.stack([row_block] * axis_size('shard'), 0), concat_axis=0,...  95.4 us
    ppermute x16, waiting for transfers between devices, shifted(): lax.ppermute(value, axis, [(source, source + steps) for source in range(i...  78.6 us
    gather x2, local copies, waits for them, and re-layouts, mode_tables(): kernel[jnp.clip(offsets, 0, block_len - 1)]  63.8 us
    ppermute x16, starting transfers between devices, shifted(): lax.ppermute(value, axis, [(source, source + steps) for source in range(i...  33.7 us
    all_to_all x1, starting transfers between devices, project_rows(): all_to_all(jnp.stack([row_block] * axis_size('shard'), 0), concat_axis=0,...  16.6 us
    dot_general x1, matrix products, shards(): intra = jnp.einsum('tsc,bsc->btc', toeplitz, blocks, precision=highest)  15.4 us
  transfers between devices with their start and end apart: 17, of which 16 were waited for; matrix products, arithmetic and copies ran while one was open for 21% of the time, Pallas kernels for 0%

profile of v1, /device:TPU:38, one launch (start us, length us, event | category | flops | bytes accessed | tf_op | source)
XLA Modules:
  0.0 320.5 jit_solution(18287305164412612240)
XLA Ops:
  0.0 0.9 copy.27
  1.0 1.6 stack.2
  2.5 16.6 %all-to-all-start = ((bf16[32,256,128]{1,2,0:T(8,128)(2,1)}), bf16[32,256,128]{1,2,0:T(8,128)(2,1)}, u32[]{:S(2)}, u32[]{:S(2)}) async-start(bf16[32,256,128]{1,2,0:T(8,128)(2,1)} %stack.2), calls=%async_computation | async-start | bytes 4194304 | tf_op jit(solution)/shard_map/all_to_all | solution.py:34
  19.1 2.8 copy.28
  22.2 0.7 dynamic-slice_bitcast_fusion.2
  23.0 0.6 multiply_reduce_fusion
  23.7 95.4 %all-to-all-done = bf16[32,256,128]{1,2,0:T(8,128)(2,1)} async-done(((bf16[32,256,128]{1,2,0:T(8,128)(2,1)}), bf16[32,256,128]{1,2,0:T(8,128)(2,1)}, u32[]{:S(2)}, u32[]{:S(2)}) %all-to-all-start) | async-done | bytes 2097184 | tf_op jit(solution)/shard_map/all_to_all | solution.py:34
  119.1 3.8 %convolution_convert_fusion = bf16[256,384]{1,0:T(8,128)(2,1)S(1)} fusion(bf16[256,4096]{0,1:T(8,128)(2,1)} %bitcast.2, bf16[4096,384]{0,1:T(8,128)(2,1)} %bitcast.52), kind=kOutput, calls=%fused_computation.8 | convolution fusion | flops 805404672 | bytes 5439488 | tf_op jit(solution)/shard_map/dot_general | solution.py:32
  123.0 2.1 collective-permute-start.1
  125.2 54.5 %gather_fusion = f32[16384,128]{1,0:T(8,128)} fusion(f32[128,128]{1,0:T(8,128)S(1)} %copy.33, s32[16384]{0:T(1024)S(1)} %fusion.23), kind=kCustom, calls=%fused_computation | custom fusion | bytes 16842752 | tf_op jit(solution)/shard_map/gather | solution.py:23
  179.7 9.3 %copy.34 = f32[128,128,128]{1,0,2:T(8,128)} copy(f32[128,128,128]{2,1,0:T(8,128)} %bitcast.51) | data formatting | bytes 16777216 | tf_op jit(solution)/shard_map/gather | solution.py:23
  189.2 0.2 copy.30
  189.5 0.4 fusion.18
  190.1 1.9 convolution_bitcast_fusion
  192.1 110.5 %while.23 = (s32[]{:T(128)}, f32[16,128]{1,0:T(8,128)S(1)}, f32[16,128]{1,0:T(8,128)S(1)}, f32[16,128]{1,0:T(8,128)S(1)}, s32[]{:T(128)}) while((s32[]{:T(128)}, f32[16,128]{1,0:T(8,128)S(1)}, f32[16,128]{1,0:T(8,128)S(1)}, f32[16,128]{1,0:T(8,128)S(1)}, s32[]{:T(128)}) %tuple.46), condition=%wide.region_4.5_spmd, body=%wide.region_3.4_spmd.sunk | while | flops 4098 | bytes 65637 | solution.py:86
  192.1 4.9 %collective-permute-start = (f32[16,128]{1,0:T(8,128)S(1)}, f32[16,128]{1,0:T(8,128)S(1)}, u32[]{:S(2)}, u32[]{:S(2)}) collective-permute-start(f32[16,128]{1,0:T(8,128)S(1)} %multiply_add_fusion.3), channel_id=1, source_target_pairs={{0,32},{32,64},{64,96},{96,128},{128,160},{160,192},{192,224},{224... | collective-permute-start | bytes 24584 | tf_op jit(solution)/shard_map/while/body/eval_jaxpr/ppermute | solution.py:12
  197.0 2.5 collective-permute-done
  199.5 1.9 collective-permute-start
  201.4 5.4 %collective-permute-done = f32[16,128]{1,0:T(8,128)S(1)} collective-permute-done((f32[16,128]{1,0:T(8,128)S(1)}, f32[16,128]{1,0:T(8,128)S(1)}, u32[]{:S(2)}, u32[]{:S(2)}) %collective-permute-start) | collective-permute-done | bytes 8224 | tf_op jit(solution)/shard_map/while/body/eval_jaxpr/ppermute | solution.py:12
  206.9 1.9 collective-permute-start
  208.8 5.4 %collective-permute-done = f32[16,128]{1,0:T(8,128)S(1)} collective-permute-done((f32[16,128]{1,0:T(8,128)S(1)}, f32[16,128]{1,0:T(8,128)S(1)}, u32[]{:S(2)}, u32[]{:S(2)}) %collective-permute-start) | collective-permute-done | bytes 8224 | tf_op jit(solution)/shard_map/while/body/eval_jaxpr/ppermute | solution.py:12
  214.2 1.9 collective-permute-start
  216.1 5.4 %collective-permute-done = f32[16,128]{1,0:T(8,128)S(1)} collective-permute-done((f32[16,128]{1,0:T(8,128)S(1)}, f32[16,128]{1,0:T(8,128)S(1)}, u32[]{:S(2)}, u32[]{:S(2)}) %collective-permute-start) | collective-permute-done | bytes 8224 | tf_op jit(solution)/shard_map/while/body/eval_jaxpr/ppermute | solution.py:12
  221.6 1.9 collective-permute-start
  223.5 5.4 %collective-permute-done = f32[16,128]{1,0:T(8,128)S(1)} collective-permute-done((f32[16,128]{1,0:T(8,128)S(1)}, f32[16,128]{1,0:T(8,128)S(1)}, u32[]{:S(2)}, u32[]{:S(2)}) %collective-permute-start) | collective-permute-done | bytes 8224 | tf_op jit(solution)/shard_map/while/body/eval_jaxpr/ppermute | solution.py:12
  229.0 1.9 collective-permute-start
  230.9 5.4 %collective-permute-done = f32[16,128]{1,0:T(8,128)S(1)} collective-permute-done((f32[16,128]{1,0:T(8,128)S(1)}, f32[16,128]{1,0:T(8,128)S(1)}, u32[]{:S(2)}, u32[]{:S(2)}) %collective-permute-start) | collective-permute-done | bytes 8224 | tf_op jit(solution)/shard_map/while/body/eval_jaxpr/ppermute | solution.py:12
  236.3 1.9 collective-permute-start
  238.2 5.4 %collective-permute-done = f32[16,128]{1,0:T(8,128)S(1)} collective-permute-done((f32[16,128]{1,0:T(8,128)S(1)}, f32[16,128]{1,0:T(8,128)S(1)}, u32[]{:S(2)}, u32[]{:S(2)}) %collective-permute-start) | collective-permute-done | bytes 8224 | tf_op jit(solution)/shard_map/while/body/eval_jaxpr/ppermute | solution.py:12
  243.7 1.9 collective-permute-start
  245.6 5.4 %collective-permute-done = f32[16,128]{1,0:T(8,128)S(1)} collective-permute-done((f32[16,128]{1,0:T(8,128)S(1)}, f32[16,128]{1,0:T(8,128)S(1)}, u32[]{:S(2)}, u32[]{:S(2)}) %collective-permute-start) | collective-permute-done | bytes 8224 | tf_op jit(solution)/shard_map/while/body/eval_jaxpr/ppermute | solution.py:12
  251.1 1.9 collective-permute-start
  253.0 5.4 %collective-permute-done = f32[16,128]{1,0:T(8,128)S(1)} collective-permute-done((f32[16,128]{1,0:T(8,128)S(1)}, f32[16,128]{1,0:T(8,128)S(1)}, u32[]{:S(2)}, u32[]{:S(2)}) %collective-permute-start) | collective-permute-done | bytes 8224 | tf_op jit(solution)/shard_map/while/body/eval_jaxpr/ppermute | solution.py:12
  258.4 1.9 collective-permute-start
  260.3 5.4 %collective-permute-done = f32[16,128]{1,0:T(8,128)S(1)} collective-permute-done((f32[16,128]{1,0:T(8,128)S(1)}, f32[16,128]{1,0:T(8,128)S(1)}, u32[]{:S(2)}, u32[]{:S(2)}) %collective-permute-start) | collective-permute-done | bytes 8224 | tf_op jit(solution)/shard_map/while/body/eval_jaxpr/ppermute | solution.py:12
  265.8 1.9 collective-permute-start
  267.7 5.4 %collective-permute-done = f32[16,128]{1,0:T(8,128)S(1)} collective-permute-done((f32[16,128]{1,0:T(8,128)S(1)}, f32[16,128]{1,0:T(8,128)S(1)}, u32[]{:S(2)}, u32[]{:S(2)}) %collective-permute-start) | collective-permute-done | bytes 8224 | tf_op jit(solution)/shard_map/while/body/eval_jaxpr/ppermute | solution.py:12
  273.2 1.9 collective-permute-start
  275.1 5.4 %collective-permute-done = f32[16,128]{1,0:T(8,128)S(1)} collective-permute-done((f32[16,128]{1,0:T(8,128)S(1)}, f32[16,128]{1,0:T(8,128)S(1)}, u32[]{:S(2)}, u32[]{:S(2)}) %collective-permute-start) | collective-permute-done | bytes 8224 | tf_op jit(solution)/shard_map/while/body/eval_jaxpr/ppermute | solution.py:12
  280.5 1.9 collective-permute-start
  282.4 5.4 %collective-permute-done = f32[16,128]{1,0:T(8,128)S(1)} collective-permute-done((f32[16,128]{1,0:T(8,128)S(1)}, f32[16,128]{1,0:T(8,128)S(1)}, u32[]{:S(2)}, u32[]{:S(2)}) %collective-permute-start) | collective-permute-done | bytes 8224 | tf_op jit(solution)/shard_map/while/body/eval_jaxpr/ppermute | solution.py:12
  287.9 1.9 collective-permute-start
  289.8 5.4 %collective-permute-done = f32[16,128]{1,0:T(8,128)S(1)} collective-permute-done((f32[16,128]{1,0:T(8,128)S(1)}, f32[16,128]{1,0:T(8,128)S(1)}, u32[]{:S(2)}, u32[]{:S(2)}) %collective-permute-start) | collective-permute-done | bytes 8224 | tf_op jit(solution)/shard_map/while/body/eval_jaxpr/ppermute | solution.py:12
  295.3 1.9 collective-permute-start
  297.2 5.4 %collective-permute-done = f32[16,128]{1,0:T(8,128)S(1)} collective-permute-done((f32[16,128]{1,0:T(8,128)S(1)}, f32[16,128]{1,0:T(8,128)S(1)}, u32[]{:S(2)}, u32[]{:S(2)}) %collective-permute-start) | collective-permute-done | bytes 8224 | tf_op jit(solution)/shard_map/while/body/eval_jaxpr/ppermute | solution.py:12
  302.8 1.4 fusion.7
  304.2 15.4 %fusion.4 = f32[128,2,128]{2,1,0:T(2,128)S(1)} fusion(f32[128,2,128]{2,1,0:T(2,128)S(1)} %fusion.7, f32[2,128,128]{1,0,2:T(2,128)S(1)} %mul.171, f32[128,128,128]{1,0,2:T(8,128)} %copy.34, pred[128,128]{1,0:T(8,128)(4,1)S(1)} %subtract_compare_fusion), kind=kOutput, calls=%fused_computation.9 | convolution fusion | flops 52461568 | bytes 8798208 | tf_op jit(solution)/shard_map/tsc,bsc->btc/dot_general | solution.py:74
  319.8 0.7 copy.37
  (51 shorter events, 1.4 us)
Async XLA Ops:
  0.9 18.2 %copy-start = (bf16[4096,3,128]{2,0,1:T(8,128)(2,1)S(1)}, bf16[4096,3,128]{2,0,1:T(8,128)(2,1)}, u32[]{:S(2)}) copy-start(bf16[4096,3,128]{2,0,1:T(8,128)(2,1)} %param.11) | copy-start | bytes 9437188
  2.5 116.6 %all-to-all-start = ((bf16[32,256,128]{1,2,0:T(8,128)(2,1)}), bf16[32,256,128]{1,2,0:T(8,128)(2,1)}, u32[]{:S(2)}, u32[]{:S(2)}) async-start(bf16[32,256,128]{1,2,0:T(8,128)(2,1)} %stack.2), calls=%async_computation | async-start | bytes 4194304 | tf_op jit(solution)/shard_map/all_to_all | solution.py:34
  19.1 2.9 copy-start.1
  19.1 2.9 copy-start.2
  123.0 66.2 %collective-permute-start.1 = (bf16[2,3,128]{2,1,0:T(4,128)(2,1)S(1)}, bf16[2,3,128]{2,1,0:T(4,128)(2,1)S(1)}, u32[]{:S(2)}, u32[]{:S(2)}) collective-permute-start(bf16[2,3,128]{2,1,0:T(4,128)(2,1)S(1)} %slice.35), channel_id=1, source_target_pairs={{0,32},{32,64},{64,96},{96,128},{128,160},{160,192},{192,224},{224... | collective-permute-start | bytes 4616 | tf_op jit(solution)/shard_map/ppermute | solution.py:12
  192.1 7.4 %collective-permute-start = (f32[16,128]{1,0:T(8,128)S(1)}, f32[16,128]{1,0:T(8,128)S(1)}, u32[]{:S(2)}, u32[]{:S(2)}) collective-permute-start(f32[16,128]{1,0:T(8,128)S(1)} %multiply_add_fusion.3), channel_id=1, source_target_pairs={{0,32},{32,64},{64,96},{96,128},{128,160},{160,192},{192,224},{224... | collective-permute-start | bytes 24584 | tf_op jit(solution)/shard_map/while/body/eval_jaxpr/ppermute | solution.py:12
  199.5 7.4 %collective-permute-start = (f32[16,128]{1,0:T(8,128)S(1)}, f32[16,128]{1,0:T(8,128)S(1)}, u32[]{:S(2)}, u32[]{:S(2)}) collective-permute-start(f32[16,128]{1,0:T(8,128)S(1)} %multiply_add_fusion.3), channel_id=1, source_target_pairs={{0,32},{32,64},{64,96},{96,128},{128,160},{160,192},{192,224},{224... | collective-permute-start | bytes 24584 | tf_op jit(solution)/shard_map/while/body/eval_jaxpr/ppermute | solution.py:12
  206.9 7.4 %collective-permute-start = (f32[16,128]{1,0:T(8,128)S(1)}, f32[16,128]{1,0:T(8,128)S(1)}, u32[]{:S(2)}, u32[]{:S(2)}) collective-permute-start(f32[16,128]{1,0:T(8,128)S(1)} %multiply_add_fusion.3), channel_id=1, source_target_pairs={{0,32},{32,64},{64,96},{96,128},{128,160},{160,192},{192,224},{224... | collective-permute-start | bytes 24584 | tf_op jit(solution)/shard_map/while/body/eval_jaxpr/ppermute | solution.py:12
  214.2 7.4 %collective-permute-start = (f32[16,128]{1,0:T(8,128)S(1)}, f32[16,128]{1,0:T(8,128)S(1)}, u32[]{:S(2)}, u32[]{:S(2)}) collective-permute-start(f32[16,128]{1,0:T(8,128)S(1)} %multiply_add_fusion.3), channel_id=1, source_target_pairs={{0,32},{32,64},{64,96},{96,128},{128,160},{160,192},{192,224},{224... | collective-permute-start | bytes 24584 | tf_op jit(solution)/shard_map/while/body/eval_jaxpr/ppermute | solution.py:12
  221.6 7.4 %collective-permute-start = (f32[16,128]{1,0:T(8,128)S(1)}, f32[16,128]{1,0:T(8,128)S(1)}, u32[]{:S(2)}, u32[]{:S(2)}) collective-permute-start(f32[16,128]{1,0:T(8,128)S(1)} %multiply_add_fusion.3), channel_id=1, source_target_pairs={{0,32},{32,64},{64,96},{96,128},{128,160},{160,192},{192,224},{224... | collective-permute-start | bytes 24584 | tf_op jit(solution)/shard_map/while/body/eval_jaxpr/ppermute | solution.py:12
  229.0 7.4 %collective-permute-start = (f32[16,128]{1,0:T(8,128)S(1)}, f32[16,128]{1,0:T(8,128)S(1)}, u32[]{:S(2)}, u32[]{:S(2)}) collective-permute-start(f32[16,128]{1,0:T(8,128)S(1)} %multiply_add_fusion.3), channel_id=1, source_target_pairs={{0,32},{32,64},{64,96},{96,128},{128,160},{160,192},{192,224},{224... | collective-permute-start | bytes 24584 | tf_op jit(solution)/shard_map/while/body/eval_jaxpr/ppermute | solution.py:12
  236.3 7.4 %collective-permute-start = (f32[16,128]{1,0:T(8,128)S(1)}, f32[16,128]{1,0:T(8,128)S(1)}, u32[]{:S(2)}, u32[]{:S(2)}) collective-permute-start(f32[16,128]{1,0:T(8,128)S(1)} %multiply_add_fusion.3), channel_id=1, source_target_pairs={{0,32},{32,64},{64,96},{96,128},{128,160},{160,192},{192,224},{224... | collective-permute-start | bytes 24584 | tf_op jit(solution)/shard_map/while/body/eval_jaxpr/ppermute | solution.py:12
  243.7 7.4 %collective-permute-start = (f32[16,128]{1,0:T(8,128)S(1)}, f32[16,128]{1,0:T(8,128)S(1)}, u32[]{:S(2)}, u32[]{:S(2)}) collective-permute-start(f32[16,128]{1,0:T(8,128)S(1)} %multiply_add_fusion.3), channel_id=1, source_target_pairs={{0,32},{32,64},{64,96},{96,128},{128,160},{160,192},{192,224},{224... | collective-permute-start | bytes 24584 | tf_op jit(solution)/shard_map/while/body/eval_jaxpr/ppermute | solution.py:12
  251.1 7.4 %collective-permute-start = (f32[16,128]{1,0:T(8,128)S(1)}, f32[16,128]{1,0:T(8,128)S(1)}, u32[]{:S(2)}, u32[]{:S(2)}) collective-permute-start(f32[16,128]{1,0:T(8,128)S(1)} %multiply_add_fusion.3), channel_id=1, source_target_pairs={{0,32},{32,64},{64,96},{96,128},{128,160},{160,192},{192,224},{224... | collective-permute-start | bytes 24584 | tf_op jit(solution)/shard_map/while/body/eval_jaxpr/ppermute | solution.py:12
  258.4 7.4 %collective-permute-start = (f32[16,128]{1,0:T(8,128)S(1)}, f32[16,128]{1,0:T(8,128)S(1)}, u32[]{:S(2)}, u32[]{:S(2)}) collective-permute-start(f32[16,128]{1,0:T(8,128)S(1)} %multiply_add_fusion.3), channel_id=1, source_target_pairs={{0,32},{32,64},{64,96},{96,128},{128,160},{160,192},{192,224},{224... | collective-permute-start | bytes 24584 | tf_op jit(solution)/shard_map/while/body/eval_jaxpr/ppermute | solution.py:12
  265.8 7.4 %collective-permute-start = (f32[16,128]{1,0:T(8,128)S(1)}, f32[16,128]{1,0:T(8,128)S(1)}, u32[]{:S(2)}, u32[]{:S(2)}) collective-permute-start(f32[16,128]{1,0:T(8,128)S(1)} %multiply_add_fusion.3), channel_id=1, source_target_pairs={{0,32},{32,64},{64,96},{96,128},{128,160},{160,192},{192,224},{224... | collective-permute-start | bytes 24584 | tf_op jit(solution)/shard_map/while/body/eval_jaxpr/ppermute | solution.py:12
  273.2 7.4 %collective-permute-start = (f32[16,128]{1,0:T(8,128)S(1)}, f32[16,128]{1,0:T(8,128)S(1)}, u32[]{:S(2)}, u32[]{:S(2)}) collective-permute-start(f32[16,128]{1,0:T(8,128)S(1)} %multiply_add_fusion.3), channel_id=1, source_target_pairs={{0,32},{32,64},{64,96},{96,128},{128,160},{160,192},{192,224},{224... | collective-permute-start | bytes 24584 | tf_op jit(solution)/shard_map/while/body/eval_jaxpr/ppermute | solution.py:12
  280.5 7.4 %collective-permute-start = (f32[16,128]{1,0:T(8,128)S(1)}, f32[16,128]{1,0:T(8,128)S(1)}, u32[]{:S(2)}, u32[]{:S(2)}) collective-permute-start(f32[16,128]{1,0:T(8,128)S(1)} %multiply_add_fusion.3), channel_id=1, source_target_pairs={{0,32},{32,64},{64,96},{96,128},{128,160},{160,192},{192,224},{224... | collective-permute-start | bytes 24584 | tf_op jit(solution)/shard_map/while/body/eval_jaxpr/ppermute | solution.py:12
  287.9 7.4 %collective-permute-start = (f32[16,128]{1,0:T(8,128)S(1)}, f32[16,128]{1,0:T(8,128)S(1)}, u32[]{:S(2)}, u32[]{:S(2)}) collective-permute-start(f32[16,128]{1,0:T(8,128)S(1)} %multiply_add_fusion.3), channel_id=1, source_target_pairs={{0,32},{32,64},{64,96},{96,128},{128,160},{160,192},{192,224},{224... | collective-permute-start | bytes 24584 | tf_op jit(solution)/shard_map/while/body/eval_jaxpr/ppermute | solution.py:12
  295.3 7.4 %collective-permute-start = (f32[16,128]{1,0:T(8,128)S(1)}, f32[16,128]{1,0:T(8,128)S(1)}, u32[]{:S(2)}, u32[]{:S(2)}) collective-permute-start(f32[16,128]{1,0:T(8,128)S(1)} %multiply_add_fusion.3), channel_id=1, source_target_pairs={{0,32},{32,64},{64,96},{96,128},{128,160},{160,192},{192,224},{224... | collective-permute-start | bytes 24584 | tf_op jit(solution)/shard_map/while/body/eval_jaxpr/ppermute | solution.py:12
  304.2 15.4 %copy-start.3 = (f32[128]{0:T(128)S(1)}, f32[128]{0:T(128)}, u32[]{:S(2)}) copy-start(f32[128]{0:T(128)} %param.15) | copy-start | bytes 1540
